TPU v7x, 256 devices: a whole 4x4x8 slice. The times are simulated.
256 devices in a mesh: rep: 32 (over y, z), tp: 8 (over x, core).
Axes of the slice: x: 4, y: 4, z: 8, core: 2. Of those that a mesh axis runs over, the one named last changes fastest.
Arguments:
- reference_rows: bfloat16 [32768, 8192], P('rep', 'tp'), may hold values from -7 to 7
- critic_rows: bfloat16 [32768, 4096], P('rep', 'tp'), may hold values from -7 to 7
- segment_ids: int32 [32768], P('rep'), may hold values from -1 to 32767, as said below
- pack_dest: int32 [32, 32], P('rep'), may hold values from 0 to 31, as said below
- ref_query: bfloat16 [8192, 4096], P('rep', 'tp'), may hold values from -2 to 2
- ref_key: bfloat16 [8192, 1024], P('rep', 'tp'), may hold values from -2 to 2
- ref_value: bfloat16 [8192, 1024], P('rep', 'tp'), may hold values from -0.0625 to 0.0625
- critic_query: bfloat16 [4096, 4096], P(None, 'tp'), may hold values from -2 to 2
- critic_key: bfloat16 [4096, 1024], P(None, 'tp'), may hold values from -2 to 2
- critic_value: bfloat16 [4096, 1024], P(None, 'tp'), may hold values from -0.09375 to 0.09375
- ref_readout: bfloat16 [4096], P('tp'), may hold values from -0.09375 to 0.09375
- critic_readout: bfloat16 [4096], P('tp'), may hold values from -0.09375 to 0.09375
Outputs:
- ref_score: float32 [32768], P('rep')
- value: float32 [32768], P('rep')
Inputs may be any that keep to these rules, and one draw needn't show every extreme that they name: Each row is a permutation: block b of replica s goes to pack pack_dest[s, b]. `segment_ids`: in every aligned block of 32 slots the used rows come first and the rest hold -1; a block holds 1 to 31 used rows, and every pack receives exactly 31 used rows from some replica and exactly 512 used rows in all. A rollout is a run of consecutive used rows with one id inside one block; different rollouts have different ids.
All inputs are finite; a program needn't handle non-finite values.
Results may differ from a plain program's by a relative error of at most 0.0084.
Values may be sent and summed in bfloat16 or wider, within the bound.
No kernel may reach another device: no remote copies, remote signals or barrier semaphores. Data moves between devices by JAX's collectives and lax.ppermute only.
A program may use at most 128 MiB of HBM per device.

v0:
```python
import jax
import jax.numpy as jnp
from jax import lax
from jax.sharding import PartitionSpec as P

HD = 128


def normalize(source):
    widened = source.astype(jnp.float32)
    scale_row = lax.rsqrt(jnp.mean(widened * widened, axis=-1, keepdims=True) + 1e-05)
    return (widened * scale_row).astype(jnp.bfloat16)


def attend(queries, keys_in, values_in, segments):
    row_count = queries.shape[0]
    groups = keys_in.shape[1] // HD
    shared = queries.shape[1] // keys_in.shape[1]
    query_four = queries.reshape(row_count, groups, shared, HD)
    key_three = keys_in.reshape(row_count, groups, HD)
    value_three = values_in.reshape(row_count, groups, HD)
    scores = jnp.einsum(
        "pgjd,qgd->gjpq", query_four, key_three, preferred_element_type=jnp.float32
    ) * HD ** (-0.5)
    position = jnp.arange(row_count)
    allowed = (position[None, :] <= position[:, None]) & (segments[:, None] == segments[None, :])
    masked = jnp.where(allowed, scores, -1e30)
    row_max = jnp.max(masked, axis=-1, keepdims=True)
    powers = jnp.where(allowed, jnp.exp(masked - row_max), 0.0)
    weights = (powers / jnp.sum(powers, axis=-1, keepdims=True)).astype(jnp.bfloat16)
    mixture = jnp.einsum("gjpq,qgd->pgjd", weights, value_three, preferred_element_type=jnp.float32)
    return mixture.reshape(row_count, groups * shared * HD).astype(jnp.bfloat16)


def compact_index(segments):
    row_count = segments.shape[0]
    sort_keys = jnp.where(segments >= 0, 0, row_count).astype(jnp.int32) + jnp.arange(
        row_count, dtype=jnp.int32
    )
    return jnp.argsort(sort_keys)[: row_count // 2]


def project(normed, weight):
    return jnp.dot(normed, weight, preferred_element_type=jnp.float32).astype(jnp.bfloat16)


def body(
    reference_rows,
    critic_rows,
    segment_ids,
    pack_dest,
    ref_query,
    ref_key,
    ref_value,
    critic_query,
    critic_key,
    critic_value,
    ref_readout,
    critic_readout,
):
    replicas = lax.axis_size("rep")
    slot_count = segment_ids.shape[0]
    block_rows = slot_count // replicas
    destination = pack_dest[0]
    inverse = jnp.argsort(destination)

    def by_pack(source):
        blocks = source.reshape((replicas, block_rows) + source.shape[1:])
        return jnp.take(blocks, inverse, axis=0).reshape(source.shape)

    ref_in, critic_in, ids_in = (
        lax.all_to_all(by_pack(reference_rows), "rep", split_axis=0, concat_axis=0, tiled=True),
        lax.all_to_all(by_pack(critic_rows), "rep", split_axis=0, concat_axis=0, tiled=True),
        lax.all_to_all(by_pack(segment_ids), "rep", split_axis=0, concat_axis=0, tiled=True),
    )
    chosen = compact_index(ids_in)
    pack_ids = ids_in[chosen]
    ref_full, critic_full = (
        lax.all_gather(ref_in[chosen], "tp", axis=1, tiled=True),
        lax.all_gather(critic_in[chosen], "tp", axis=1, tiled=True),
    )
    critic_normed = normalize(critic_full)
    critic_attn = attend(
        project(critic_normed, critic_query),
        project(critic_normed, critic_key),
        project(critic_normed, critic_value),
        pack_ids,
    )
    ref_normed = normalize(ref_full)
    pieces = (
        lax.all_gather(ref_query, "rep", axis=0, tiled=True),
        lax.all_gather(ref_key, "rep", axis=0, tiled=True),
        lax.all_gather(ref_value, "rep", axis=0, tiled=True),
    )
    ref_q, ref_k, ref_v = tuple(
        (
            jnp.dot(ref_normed, weight_piece, preferred_element_type=jnp.float32)
            for weight_piece in pieces
        )
    )
    ref_attn = attend(
        ref_q.astype(jnp.bfloat16), ref_k.astype(jnp.bfloat16), ref_v.astype(jnp.bfloat16), pack_ids
    )
    ref_spread = jnp.zeros((slot_count, ref_attn.shape[1]), jnp.bfloat16).at[chosen].set(ref_attn)
    critic_spread = (
        jnp.zeros((slot_count, critic_attn.shape[1]), jnp.bfloat16).at[chosen].set(critic_attn)
    )
    ref_home, critic_home = (
        lax.all_to_all(ref_spread, "rep", split_axis=0, concat_axis=0, tiled=True),
        lax.all_to_all(critic_spread, "rep", split_axis=0, concat_axis=0, tiled=True),
    )
    ref_home = jnp.take(ref_home.reshape(replicas, block_rows, -1), destination, axis=0).reshape(
        slot_count, -1
    )
    critic_home = jnp.take(
        critic_home.reshape(replicas, block_rows, -1), destination, axis=0
    ).reshape(slot_count, -1)
    partial_value = jnp.stack(
        [
            jnp.dot(ref_home, ref_readout, preferred_element_type=jnp.float32),
            jnp.dot(critic_home, critic_readout, preferred_element_type=jnp.float32),
        ]
    )
    ordered = lax.psum(partial_value, "tp")
    ordered = jnp.where(segment_ids[None, :] >= 0, ordered, 0.0)
    return (ordered[0], ordered[1])


def solution(mesh):
    return jax.shard_map(
        body,
        mesh=mesh,
        in_specs=(
            P("rep", "tp"),
            P("rep", "tp"),
            P("rep"),
            P("rep", None),
            P("rep", "tp"),
            P("rep", "tp"),
            P("rep", "tp"),
            P(None, "tp"),
            P(None, "tp"),
            P(None, "tp"),
            P("tp"),
            P("tp"),
        ),
        out_specs=(P("rep"), P("rep")),
        check_vma=False,
    )
```

profile of v0, /device:TPU:1, one launch (start us, length us, event | category | flops | bytes accessed | tf_op | source)
XLA Modules:
  0.0 513.6 jit_solution(6631517655676095522)
XLA Ops:
  11.6 12.0 %all-to-all-start = ((s32[32,32,1]{1,2,0:T(1,128)}), s32[32,32,1]{1,2,0:T(1,128)S(1)}, u32[]{:S(2)}, u32[]{:S(2)}) async-start(s32[32,32,1]{1,2,0:T(1,128)} %bitcast.2), calls=%async_computation | async-start | bytes 32768 | tf_op jit(solution)/shard_map/all_to_all | solution.py:74
  26.7 5.6 %all-to-all-done = s32[32,32,1]{1,2,0:T(1,128)S(1)} async-done(((s32[32,32,1]{1,2,0:T(1,128)}), s32[32,32,1]{1,2,0:T(1,128)S(1)}, u32[]{:S(2)}, u32[]{:S(2)}) %all-to-all-start) | async-done | bytes 4128 | tf_op jit(solution)/shard_map/all_to_all | solution.py:74
  32.3 3.9 all-to-all-start.3
  37.6 4.4 sort.35
  41.9 18.7 %all-to-all-done.3 = bf16[32,32,512]{2,1,0:T(8,128)(2,1)S(1)} async-done(((bf16[32,32,512]{2,1,0:T(8,128)(2,1)}), bf16[32,32,512]{2,1,0:T(8,128)(2,1)S(1)}, u32[]{:S(2)}, u32[]{:S(2)}) %all-to-all-start.3) | async-done | bytes 1048608 | tf_op jit(solution)/shard_map/all_to_all | solution.py:73
  67.2 55.1 %all_to_all.45 = bf16[32,32,1024]{2,1,0:T(8,128)(2,1)} all-to-all(bf16[32,32,1024]{2,1,0:T(8,128)(2,1)S(1)} %broadcast_select_fusion), channel_id=1, replica_groups=mesh['rep'=32,'tp'=8] {'rep'}, dimensions={0} | all-to-all | bytes 4194304 | tf_op jit(solution)/shard_map/all_to_all | solution.py:72
  122.3 5.4 %gather_fusion.2 = bf16[512,1024]{1,0:T(8,128)(2,1)} fusion(bf16[1024,1024]{1,0:T(8,128)(2,1)} %bitcast.109, s32[1024]{0:T(1024)S(1)} %pad_clamp_fusion.1), kind=kCustom, calls=%fused_computation.5 | custom fusion | bytes 2099200 | tf_op jit(solution)/shard_map/gather | solution.py:79
  136.0 4.7 convolution_convert_fusion
  140.8 40.8 %all-gather.14.cloned.1.call-done = bf16[512,8192]{1,0:T(8,128)(2,1)} async-done(((bf16[512,1024]{1,0:T(8,128)(2,1)}), bf16[512,8192]{1,0:T(8,128)(2,1)}) %all-gather.14.cloned.1.call-update) | async-done | bytes 8388624 | tf_op jit(solution)/shard_map/all_gather | solution.py:79
  181.5 5.1 fusion
  186.6 95.4 %all-gather.12.cloned.1.call-done = bf16[8192,512]{1,0:T(8,128)(2,1)} async-done(((bf16[256,512]{1,0:T(8,128)(2,1)}), bf16[8192,512]{1,0:T(8,128)(2,1)}) %all-gather.12.cloned.1.call-update) | async-done | bytes 8388624 | tf_op jit(solution)/shard_map/all_gather | solution.py:91
  282.1 11.2 %convolution_convert_fusion.1 = bf16[512,512]{0,1:T(8,128)(2,1)} fusion(bf16[8192,512]{1,0:T(8,128)(2,1)} %all-gather.12.cloned.1.call-done, bf16[512,8192]{1,0:T(8,128)(2,1)} %all-gather.14.cloned.1.call-done, f32[512]{0:T(512)S(1)} %add_rsqrt_fusion.1), kind=kOutput, calls=%fused_computation.38 | convolution fusion | flops 4307812352 | bytes 17303552 | tf_op jit(solution)/shard_map/dot_general | solution.py:97
  293.3 62.8 %all-gather.10.cloned.1.call-done = bf16[8192,128]{1,0:T(8,128)(2,1)} async-done(((bf16[256,128]{1,0:T(8,128)(2,1)}), bf16[8192,128]{1,0:T(8,128)(2,1)}) %all-gather.10.cloned.1.call-update) | async-done | bytes 2097168 | tf_op jit(solution)/shard_map/all_gather | solution.py:92
  356.1 10.2 %fusion.4 = (f32[4,512]{1,0:T(4,128)S(1)}, f32[512,512,4]{1,0,2:T(8,128)}) fusion(pred[512,512]{0,1:T(8,128)(4,1)S(1)} %fusion.26, bf16[512,4,128]{0,2,1:T(8,128)(2,1)} %bitcast.122, bf16[8192,128]{1,0:T(8,128)(2,1)} %all-gather.10.cloned.1.call-done, bf16[512,8192]{1,0:T(8,128)(2,1)} %all-gather.14.cloned.1.call-done, f32[512]{0:T(512)S(1)} %add_rsqrt_fusion.1), kind=kOutput, calls=%fused_computation.24 | convolution fusion | flops 1357969408 | bytes 15476736 | tf_op jit(solution)/shard_map/pgjd,qgd->gjpq/dot_general | solution.py:22
  366.3 9.5 %fusion.6 = (f32[4,512]{1,0:T(4,128)S(1)}, f32[4,512]{1,0:T(4,128)S(1)}, f32[512,512,4]{1,0,2:T(8,128)}) fusion(f32[512,512,4]{1,0,2:T(8,128)} %get-tuple-element.14, f32[4,512]{1,0:T(4,128)S(1)} %get-tuple-element.13, pred[512,512]{0,1:T(8,128)(4,1)S(1)} %fusion.26, bf16[512,4,128]{0,2,1:T(8,128)(2,1)S(1)} %bitcast.121, bf16[4096,128]{1,0:T(8,128)(2,1)} %param.22, ...), kind=kOutput, calls=%fused_computation.26 | convolution fusion | flops 820047872 | bytes 14444544 | tf_op jit(solution)/shard_map/pgjd,qgd->gjpq/dot_general | solution.py:22
  379.0 6.6 %fusion.17 = bf16[128,4,512]{2,0,1:T(8,128)(2,1)S(1)} fusion(f32[4,512]{1,0:T(4,128)S(1)} %fusion.7, f32[4,512]{1,0:T(4,128)S(1)} %get-tuple-element.8, f32[512,512,4]{1,0,2:T(8,128)} %get-tuple-element.15, pred[512,512]{0,1:T(8,128)(4,1)S(1)} %fusion.26, bf16[4096,128]{1,0:T(8,128)(2,1)} %param.23, bf16[512,4096]{1,0:T(8,128)(2,1)} %all-gather.16.cloned.1.call-done, ...), kind=kOutput, calls=%fused_computation.37 | convolution fusion | flops 818216960 | bytes 10242048 | tf_op jit(solution)/shard_map/gjpq,qgd->pgjd/dot_general | solution.py:31
  385.8 3.5 scatter_custom_fusion.1
  389.4 5.3 %all-to-all-start.4 = ((bf16[32,32,512]{2,1,0:T(8,128)(2,1)}), bf16[32,32,512]{2,1,0:T(8,128)(2,1)S(1)}, u32[]{:S(2)}, u32[]{:S(2)}) async-start(bf16[32,32,512]{2,1,0:T(8,128)(2,1)} %bitcast.113), calls=%async_computation.4 | async-start | bytes 2097152 | tf_op jit(solution)/shard_map/all_to_all | solution.py:110
  394.7 42.2 %all-gather.8.cloned.1.call-done = bf16[8192,128]{1,0:T(8,128)(2,1)} async-done(((bf16[256,128]{1,0:T(8,128)(2,1)}), bf16[8192,128]{1,0:T(8,128)(2,1)}) %all-gather.8.cloned.1.call-update) | async-done | bytes 2097168 | tf_op jit(solution)/shard_map/all_gather | solution.py:93
  436.9 9.9 %fusion.14 = bf16[128,4,512]{2,0,1:T(8,128)(2,1)} fusion(f32[4,512]{1,0:T(4,128)S(1)} %get-tuple-element.7, f32[4,512]{1,0:T(4,128)S(1)} %get-tuple-element.13, f32[512,512,4]{1,0,2:T(8,128)} %get-tuple-element.14, pred[512,512]{0,1:T(8,128)(4,1)S(1)} %fusion.26, bf16[8192,128]{1,0:T(8,128)(2,1)} %all-gather.8.cloned.1.call-done, ...), kind=kOutput, calls=%fused_computation.36 | convolution fusion | flops 1361379328 | bytes 15484928 | tf_op jit(solution)/shard_map/gjpq,qgd->pgjd/dot_general | solution.py:31
  448.9 4.0 scatter_custom_fusion
  452.9 6.5 %all-to-all-start.2 = ((bf16[32,32,512]{2,1,0:T(8,128)(2,1)}), bf16[32,32,512]{2,1,0:T(8,128)(2,1)}, u32[]{:S(2)}, u32[]{:S(2)}) async-start(bf16[32,32,512]{2,1,0:T(8,128)(2,1)} %bitcast.114), calls=%async_computation.2 | async-start | bytes 2097152 | tf_op jit(solution)/shard_map/all_to_all | solution.py:109
  461.3 19.5 %all-to-all-done.2 = bf16[32,32,512]{2,1,0:T(8,128)(2,1)} async-done(((bf16[32,32,512]{2,1,0:T(8,128)(2,1)}), bf16[32,32,512]{2,1,0:T(8,128)(2,1)}, u32[]{:S(2)}, u32[]{:S(2)}) %all-to-all-start.2) | async-done | bytes 1048608 | tf_op jit(solution)/shard_map/all_to_all | solution.py:109
  485.9 20.3 %psum.7 = f32[2,1024]{1,0:T(2,128)S(1)} all-reduce(f32[2,1024]{1,0:T(2,128)S(1)} %pad_maximum_fusion), channel_id=1, replica_groups=mesh['rep'=32,'tp'=8] {'tp'}, use_global_device_ids=true, to_apply=%region_10.12 | all-reduce | flops 2048 | bytes 16384 | tf_op jit(solution)/shard_map/psum | solution.py:124
  (68 shorter events, 36.8 us)
Async XLA Ops:
  7.2 56.2 %copy-start = (bf16[1024,1024]{1,0:T(8,128)(2,1)S(1)}, bf16[1024,1024]{1,0:T(8,128)(2,1)}, u32[]{:S(2)}) copy-start(bf16[1024,1024]{1,0:T(8,128)(2,1)} %param.14) | copy-start | bytes 6291460
  11.6 20.7 %all-to-all-start = ((s32[32,32,1]{1,2,0:T(1,128)}), s32[32,32,1]{1,2,0:T(1,128)S(1)}, u32[]{:S(2)}, u32[]{:S(2)}) async-start(s32[32,32,1]{1,2,0:T(1,128)} %bitcast.2), calls=%async_computation | async-start | bytes 32768 | tf_op jit(solution)/shard_map/all_to_all | solution.py:74
  32.3 28.3 %all-to-all-start.3 = ((bf16[32,32,512]{2,1,0:T(8,128)(2,1)}), bf16[32,32,512]{2,1,0:T(8,128)(2,1)S(1)}, u32[]{:S(2)}, u32[]{:S(2)}) async-start(bf16[32,32,512]{2,1,0:T(8,128)(2,1)} %broadcast_select_fusion.1), calls=%async_computation.3 | async-start | bytes 2097152 | tf_op jit(solution)/shard_map/all_to_all | solution.py:73
  36.2 96.4 %all-gather.16.cloned.1.call-start = ((), (), s32[]{:S(2)}) async-start(), calls=%async_computation.9 | async-start | bytes 4718592 | tf_op jit(solution)/shard_map/all_gather | solution.py:80
  63.3 118.3 %all-gather.14.cloned.1.call-start = ((), (), s32[]{:S(2)}) async-start(), calls=%async_computation.8 | async-start | bytes 9437184 | tf_op jit(solution)/shard_map/all_gather | solution.py:79
  127.7 154.4 %all-gather.12.cloned.1.call-start = ((), (), s32[]{:S(2)}) async-start(), calls=%async_computation.7 | async-start | bytes 8650752 | tf_op jit(solution)/shard_map/all_gather | solution.py:91
  128.4 227.6 %all-gather.10.cloned.1.call-start = ((), (), s32[]{:S(2)}) async-start(), calls=%async_computation.6 | async-start | bytes 2162688 | tf_op jit(solution)/shard_map/all_gather | solution.py:92
  129.0 307.9 %all-gather.8.cloned.1.call-start = ((), (), s32[]{:S(2)}) async-start(), calls=%async_computation.5 | async-start | bytes 2162688 | tf_op jit(solution)/shard_map/all_gather | solution.py:93
  132.6 3.5 copy-start.2
  389.4 63.5 %all-to-all-start.4 = ((bf16[32,32,512]{2,1,0:T(8,128)(2,1)}), bf16[32,32,512]{2,1,0:T(8,128)(2,1)S(1)}, u32[]{:S(2)}, u32[]{:S(2)}) async-start(bf16[32,32,512]{2,1,0:T(8,128)(2,1)} %bitcast.113), calls=%async_computation.4 | async-start | bytes 2097152 | tf_op jit(solution)/shard_map/all_to_all | solution.py:110
  446.8 12.6 %copy-start.4 = (bf16[512]{0:T(512)(128)(2,1)S(1)}, bf16[512]{0:T(512)(128)(2,1)}, u32[]{:S(2)}) copy-start(bf16[512]{0:T(512)(128)(2,1)} %param.24) | copy-start | bytes 3076
  446.8 12.6 %copy-start.5 = (bf16[512]{0:T(512)(128)(2,1)S(1)}, bf16[512]{0:T(512)(128)(2,1)}, u32[]{:S(2)}) copy-start(bf16[512]{0:T(512)(128)(2,1)} %param.25) | copy-start | bytes 3076
  446.8 12.6 %copy-start.6 = (s32[1,32]{1,0:T(1,128)S(1)}, s32[1,32]{1,0:T(1,128)}, u32[]{:S(2)}) copy-start(s32[1,32]{1,0:T(1,128)} %param.17) | copy-start | bytes 388
  446.8 12.7 %copy-start.3 = (s32[1024]{0:T(1024)S(1)}, s32[1024]{0:T(1024)}, u32[]{:S(2)}) copy-start(s32[1024]{0:T(1024)} %param.16) | copy-start | bytes 12292
  452.9 6.6 %copy-start.1 = (bf16[32,32,512]{2,1,0:T(8,128)(2,1)}, bf16[32,32,512]{2,1,0:T(8,128)(2,1)S(1)}, u32[]{:S(2)}) copy-start(bf16[32,32,512]{2,1,0:T(8,128)(2,1)S(1)} %all-to-all-done.4) | copy-start | bytes 3145732
  452.9 27.9 %all-to-all-start.2 = ((bf16[32,32,512]{2,1,0:T(8,128)(2,1)}), bf16[32,32,512]{2,1,0:T(8,128)(2,1)}, u32[]{:S(2)}, u32[]{:S(2)}) async-start(bf16[32,32,512]{2,1,0:T(8,128)(2,1)} %bitcast.114), calls=%async_computation.2 | async-start | bytes 2097152 | tf_op jit(solution)/shard_map/all_to_all | solution.py:109
Sparse Core Ops, SparseCore 0:
  63.4 36.1 all-gather.15
  127.8 53.6 all-gather.13
  184.1 97.8 all-gather.11
  284.5 71.5 all-gather.9
  358.5 78.3 all-gather.7
where the time goes:
time: 519 us; the launch traced here: 514 us
  waiting for transfers between devices  287 us (55%)
  blocking collectives  75.4 us (15%)
  matrix products  52.9 us (10%)
  local copies, waits for them, and re-layouts  31.9 us (6%)
  starting transfers between devices  27.9 us (5%)
  other arithmetic  24.5 us (5%)
  between operations  14.3 us (3%)
    all_gather x1, waiting for transfers between devices, body(): lax.all_gather(ref_query, 'rep', axis=0, tiled=True)  95.4 us
    all_gather x1, waiting for transfers between devices, body(): lax.all_gather(ref_key, 'rep', axis=0, tiled=True)  62.8 us
    all_to_all x1, blocking collectives, body(): lax.all_to_all(by_pack(reference_rows), 'rep', split_axis=0, concat_axis=...  55.1 us
    all_gather x1, waiting for transfers between devices, body(): lax.all_gather(ref_value, 'rep', axis=0, tiled=True)  42.2 us
    all_gather x1, waiting for transfers between devices, body(): lax.all_gather(ref_in[chosen], 'tp', axis=1, tiled=True)  40.8 us
    psum x1, blocking collectives, body(): ordered = lax.psum(partial_value, 'tp')  20.3 us
    dot_general x2, matrix products, attend(): jnp.einsum('pgjd,qgd->gjpq', query_four, key_three, preferred_element_typ...  19.7 us
    all_to_all x1, waiting for transfers between devices, body(): lax.all_to_all(ref_spread, 'rep', split_axis=0, concat_axis=0, tiled=True)  19.5 us
  transfers between devices with their start and end apart: 9, of which 7 were waited for; matrix products, arithmetic and copies ran while one was open for 19% of the time, Pallas kernels for 0%

commit v1 on v0

--- a/solution.py
+++ b/solution.py
@@ -121,7 +121,8 @@
             jnp.dot(critic_home, critic_readout, preferred_element_type=jnp.float32),
         ]
     )
-    ordered = lax.psum(partial_value, "tp")
+    kept_arr = lax.all_gather(partial_value, "tp")
+    ordered = jnp.sum(kept_arr, 0)
     ordered = jnp.where(segment_ids[None, :] >= 0, ordered, 0.0)
     return (ordered[0], ordered[1])
 

time: 519 us -> 520 us (level)
    all_gather x0 -> x1, blocking collectives: none -> 21 us  [body(): kept_arr = lax.all_gather(partial_value, 'tp')]
    psum x1 -> x0, blocking collectives: 20.3 us -> none  [body(): ordered = lax.psum(partial_value, 'tp')]
where the time goes in v1:
time: 520 us; the launch traced here: 514 us
  waiting for transfers between devices  287 us (55%)
  blocking collectives  76.1 us (15%)
  matrix products  52.9 us (10%)
  local copies, waits for them, and re-layouts  31.9 us (6%)
  starting transfers between devices  27.9 us (5%)
  other arithmetic  24.5 us (5%)
  between operations  14.3 us (3%)
    all_gather x1, waiting for transfers between devices, body(): lax.all_gather(ref_query, 'rep', axis=0, tiled=True)  95.4 us
    all_gather x1, waiting for transfers between devices, body(): lax.all_gather(ref_key, 'rep', axis=0, tiled=True)  62.8 us
    all_to_all x1, blocking collectives, body(): lax.all_to_all(by_pack(reference_rows), 'rep', split_axis=0, concat_axis=...  55.1 us
    all_gather x1, waiting for transfers between devices, body(): lax.all_gather(ref_value, 'rep', axis=0, tiled=True)  42.2 us
    all_gather x1, waiting for transfers between devices, body(): lax.all_gather(ref_in[chosen], 'tp', axis=1, tiled=True)  40.8 us
    all_gather x1, blocking collectives, body(): kept_arr = lax.all_gather(partial_value, 'tp')  21 us
    dot_general x2, matrix products, attend(): jnp.einsum('pgjd,qgd->gjpq', query_four, key_three, preferred_element_typ...  19.7 us
    all_to_all x1, waiting for transfers between devices, body(): lax.all_to_all(ref_spread, 'rep', split_axis=0, concat_axis=0, tiled=True)  19.5 us
  transfers between devices with their start and end apart: 9, of which 7 were waited for; matrix products, arithmetic and copies ran while one was open for 19% of the time, Pallas kernels for 0%

profile of v1, /device:TPU:1, one launch (start us, length us, event | category | flops | bytes accessed | tf_op | source)
XLA Modules:
  0.0 514.3 jit_solution(6853609630676666132)
XLA Ops:
  11.6 12.0 %all-to-all-start = ((s32[32,32,1]{1,2,0:T(1,128)}), s32[32,32,1]{1,2,0:T(1,128)S(1)}, u32[]{:S(2)}, u32[]{:S(2)}) async-start(s32[32,32,1]{1,2,0:T(1,128)} %bitcast.2), calls=%async_computation | async-start | bytes 32768 | tf_op jit(solution)/shard_map/all_to_all | solution.py:74
  26.7 5.6 %all-to-all-done = s32[32,32,1]{1,2,0:T(1,128)S(1)} async-done(((s32[32,32,1]{1,2,0:T(1,128)}), s32[32,32,1]{1,2,0:T(1,128)S(1)}, u32[]{:S(2)}, u32[]{:S(2)}) %all-to-all-start) | async-done | bytes 4128 | tf_op jit(solution)/shard_map/all_to_all | solution.py:74
  32.3 3.9 all-to-all-start.3
  37.6 4.4 sort.35
  41.9 18.7 %all-to-all-done.3 = bf16[32,32,512]{2,1,0:T(8,128)(2,1)S(1)} async-done(((bf16[32,32,512]{2,1,0:T(8,128)(2,1)}), bf16[32,32,512]{2,1,0:T(8,128)(2,1)S(1)}, u32[]{:S(2)}, u32[]{:S(2)}) %all-to-all-start.3) | async-done | bytes 1048608 | tf_op jit(solution)/shard_map/all_to_all | solution.py:73
  67.2 55.1 %all_to_all.45 = bf16[32,32,1024]{2,1,0:T(8,128)(2,1)} all-to-all(bf16[32,32,1024]{2,1,0:T(8,128)(2,1)S(1)} %broadcast_select_fusion), channel_id=1, replica_groups=mesh['rep'=32,'tp'=8] {'rep'}, dimensions={0} | all-to-all | bytes 4194304 | tf_op jit(solution)/shard_map/all_to_all | solution.py:72
  122.3 5.4 %gather_fusion.2 = bf16[512,1024]{1,0:T(8,128)(2,1)} fusion(bf16[1024,1024]{1,0:T(8,128)(2,1)} %bitcast.111, s32[1024]{0:T(1024)S(1)} %pad_clamp_fusion.1), kind=kCustom, calls=%fused_computation.5 | custom fusion | bytes 2099200 | tf_op jit(solution)/shard_map/gather | solution.py:79
  136.0 4.7 convolution_convert_fusion
  140.8 40.8 %all-gather.16.cloned.1.call-done = bf16[512,8192]{1,0:T(8,128)(2,1)} async-done(((bf16[512,1024]{1,0:T(8,128)(2,1)}), bf16[512,8192]{1,0:T(8,128)(2,1)}) %all-gather.16.cloned.1.call-update) | async-done | bytes 8388624 | tf_op jit(solution)/shard_map/all_gather | solution.py:79
  181.5 5.1 fusion
  186.6 95.4 %all-gather.14.cloned.1.call-done = bf16[8192,512]{1,0:T(8,128)(2,1)} async-done(((bf16[256,512]{1,0:T(8,128)(2,1)}), bf16[8192,512]{1,0:T(8,128)(2,1)}) %all-gather.14.cloned.1.call-update) | async-done | bytes 8388624 | tf_op jit(solution)/shard_map/all_gather | solution.py:91
  282.1 11.2 %convolution_convert_fusion.1 = bf16[512,512]{0,1:T(8,128)(2,1)} fusion(bf16[8192,512]{1,0:T(8,128)(2,1)} %all-gather.14.cloned.1.call-done, bf16[512,8192]{1,0:T(8,128)(2,1)} %all-gather.16.cloned.1.call-done, f32[512]{0:T(512)S(1)} %add_rsqrt_fusion.1), kind=kOutput, calls=%fused_computation.38 | convolution fusion | flops 4307812352 | bytes 17303552 | tf_op jit(solution)/shard_map/dot_general | solution.py:97
  293.3 62.8 %all-gather.12.cloned.1.call-done = bf16[8192,128]{1,0:T(8,128)(2,1)} async-done(((bf16[256,128]{1,0:T(8,128)(2,1)}), bf16[8192,128]{1,0:T(8,128)(2,1)}) %all-gather.12.cloned.1.call-update) | async-done | bytes 2097168 | tf_op jit(solution)/shard_map/all_gather | solution.py:92
  356.1 10.2 %fusion.4 = (f32[4,512]{1,0:T(4,128)S(1)}, f32[512,512,4]{1,0,2:T(8,128)}) fusion(pred[512,512]{0,1:T(8,128)(4,1)S(1)} %fusion.26, bf16[512,4,128]{0,2,1:T(8,128)(2,1)} %bitcast.124, bf16[8192,128]{1,0:T(8,128)(2,1)} %all-gather.12.cloned.1.call-done, bf16[512,8192]{1,0:T(8,128)(2,1)} %all-gather.16.cloned.1.call-done, f32[512]{0:T(512)S(1)} %add_rsqrt_fusion.1), kind=kOutput, calls=%fused_computation.24 | convolution fusion | flops 1357969408 | bytes 15476736 | tf_op jit(solution)/shard_map/pgjd,qgd->gjpq/dot_general | solution.py:22
  366.3 9.5 %fusion.6 = (f32[4,512]{1,0:T(4,128)S(1)}, f32[4,512]{1,0:T(4,128)S(1)}, f32[512,512,4]{1,0,2:T(8,128)}) fusion(f32[512,512,4]{1,0,2:T(8,128)} %get-tuple-element.14, f32[4,512]{1,0:T(4,128)S(1)} %get-tuple-element.13, pred[512,512]{0,1:T(8,128)(4,1)S(1)} %fusion.26, bf16[512,4,128]{0,2,1:T(8,128)(2,1)S(1)} %bitcast.123, bf16[4096,128]{1,0:T(8,128)(2,1)} %param.22, ...), kind=kOutput, calls=%fused_computation.26 | convolution fusion | flops 820047872 | bytes 14444544 | tf_op jit(solution)/shard_map/pgjd,qgd->gjpq/dot_general | solution.py:22
  379.0 6.6 %fusion.17 = bf16[128,4,512]{2,0,1:T(8,128)(2,1)S(1)} fusion(f32[4,512]{1,0:T(4,128)S(1)} %fusion.7, f32[4,512]{1,0:T(4,128)S(1)} %get-tuple-element.8, f32[512,512,4]{1,0,2:T(8,128)} %get-tuple-element.15, pred[512,512]{0,1:T(8,128)(4,1)S(1)} %fusion.26, bf16[4096,128]{1,0:T(8,128)(2,1)} %param.23, bf16[512,4096]{1,0:T(8,128)(2,1)} %all-gather.18.cloned.1.call-done, ...), kind=kOutput, calls=%fused_computation.37 | convolution fusion | flops 818216960 | bytes 10242048 | tf_op jit(solution)/shard_map/gjpq,qgd->pgjd/dot_general | solution.py:31
  385.8 3.5 scatter_custom_fusion.1
  389.4 5.3 %all-to-all-start.4 = ((bf16[32,32,512]{2,1,0:T(8,128)(2,1)}), bf16[32,32,512]{2,1,0:T(8,128)(2,1)S(1)}, u32[]{:S(2)}, u32[]{:S(2)}) async-start(bf16[32,32,512]{2,1,0:T(8,128)(2,1)} %bitcast.115), calls=%async_computation.4 | async-start | bytes 2097152 | tf_op jit(solution)/shard_map/all_to_all | solution.py:110
  394.7 42.2 %all-gather.10.cloned.1.call-done = bf16[8192,128]{1,0:T(8,128)(2,1)} async-done(((bf16[256,128]{1,0:T(8,128)(2,1)}), bf16[8192,128]{1,0:T(8,128)(2,1)}) %all-gather.10.cloned.1.call-update) | async-done | bytes 2097168 | tf_op jit(solution)/shard_map/all_gather | solution.py:93
  436.9 9.9 %fusion.14 = bf16[128,4,512]{2,0,1:T(8,128)(2,1)} fusion(f32[4,512]{1,0:T(4,128)S(1)} %get-tuple-element.7, f32[4,512]{1,0:T(4,128)S(1)} %get-tuple-element.13, f32[512,512,4]{1,0,2:T(8,128)} %get-tuple-element.14, pred[512,512]{0,1:T(8,128)(4,1)S(1)} %fusion.26, bf16[8192,128]{1,0:T(8,128)(2,1)} %all-gather.10.cloned.1.call-done, ...), kind=kOutput, calls=%fused_computation.36 | convolution fusion | flops 1361379328 | bytes 15484928 | tf_op jit(solution)/shard_map/gjpq,qgd->pgjd/dot_general | solution.py:31
  448.9 4.0 scatter_custom_fusion
  452.9 6.5 %all-to-all-start.2 = ((bf16[32,32,512]{2,1,0:T(8,128)(2,1)}), bf16[32,32,512]{2,1,0:T(8,128)(2,1)}, u32[]{:S(2)}, u32[]{:S(2)}) async-start(bf16[32,32,512]{2,1,0:T(8,128)(2,1)} %bitcast.116), calls=%async_computation.2 | async-start | bytes 2097152 | tf_op jit(solution)/shard_map/all_to_all | solution.py:109
  461.3 19.5 %all-to-all-done.2 = bf16[32,32,512]{2,1,0:T(8,128)(2,1)} async-done(((bf16[32,32,512]{2,1,0:T(8,128)(2,1)}), bf16[32,32,512]{2,1,0:T(8,128)(2,1)}, u32[]{:S(2)}, u32[]{:S(2)}) %all-to-all-start.2) | async-done | bytes 1048608 | tf_op jit(solution)/shard_map/all_to_all | solution.py:109
  485.9 21.0 %all-gather.3 = f32[8,2,1024]{2,1,0:T(2,128)S(1)} all-gather(f32[1,2,1024]{2,1,0:T(2,128)S(1)} %maximum_bitcast_fusion), channel_id=4, replica_groups=mesh['rep'=32,'tp'=8] {'tp'}, dimensions={0}, use_global_device_ids=true | all-gather | bytes 73728 | tf_op jit(solution)/shard_map/all_gather | solution.py:124
  (69 shorter events, 36.8 us)
Async XLA Ops:
  7.2 56.2 %copy-start = (bf16[1024,1024]{1,0:T(8,128)(2,1)S(1)}, bf16[1024,1024]{1,0:T(8,128)(2,1)}, u32[]{:S(2)}) copy-start(bf16[1024,1024]{1,0:T(8,128)(2,1)} %param.14) | copy-start | bytes 6291460
  11.6 20.7 %all-to-all-start = ((s32[32,32,1]{1,2,0:T(1,128)}), s32[32,32,1]{1,2,0:T(1,128)S(1)}, u32[]{:S(2)}, u32[]{:S(2)}) async-start(s32[32,32,1]{1,2,0:T(1,128)} %bitcast.2), calls=%async_computation | async-start | bytes 32768 | tf_op jit(solution)/shard_map/all_to_all | solution.py:74
  32.3 28.3 %all-to-all-start.3 = ((bf16[32,32,512]{2,1,0:T(8,128)(2,1)}), bf16[32,32,512]{2,1,0:T(8,128)(2,1)S(1)}, u32[]{:S(2)}, u32[]{:S(2)}) async-start(bf16[32,32,512]{2,1,0:T(8,128)(2,1)} %broadcast_select_fusion.1), calls=%async_computation.3 | async-start | bytes 2097152 | tf_op jit(solution)/shard_map/all_to_all | solution.py:73
  36.2 96.4 %all-gather.18.cloned.1.call-start = ((), (), s32[]{:S(2)}) async-start(), calls=%async_computation.9 | async-start | bytes 4718592 | tf_op jit(solution)/shard_map/all_gather | solution.py:80
  63.3 118.3 %all-gather.16.cloned.1.call-start = ((), (), s32[]{:S(2)}) async-start(), calls=%async_computation.8 | async-start | bytes 9437184 | tf_op jit(solution)/shard_map/all_gather | solution.py:79
  127.7 154.4 %all-gather.14.cloned.1.call-start = ((), (), s32[]{:S(2)}) async-start(), calls=%async_computation.7 | async-start | bytes 8650752 | tf_op jit(solution)/shard_map/all_gather | solution.py:91
  128.4 227.6 %all-gather.12.cloned.1.call-start = ((), (), s32[]{:S(2)}) async-start(), calls=%async_computation.6 | async-start | bytes 2162688 | tf_op jit(solution)/shard_map/all_gather | solution.py:92
  129.0 307.9 %all-gather.10.cloned.1.call-start = ((), (), s32[]{:S(2)}) async-start(), calls=%async_computation.5 | async-start | bytes 2162688 | tf_op jit(solution)/shard_map/all_gather | solution.py:93
  132.6 3.5 copy-start.2
  389.4 63.5 %all-to-all-start.4 = ((bf16[32,32,512]{2,1,0:T(8,128)(2,1)}), bf16[32,32,512]{2,1,0:T(8,128)(2,1)S(1)}, u32[]{:S(2)}, u32[]{:S(2)}) async-start(bf16[32,32,512]{2,1,0:T(8,128)(2,1)} %bitcast.115), calls=%async_computation.4 | async-start | bytes 2097152 | tf_op jit(solution)/shard_map/all_to_all | solution.py:110
  446.8 12.6 %copy-start.4 = (bf16[512]{0:T(512)(128)(2,1)S(1)}, bf16[512]{0:T(512)(128)(2,1)}, u32[]{:S(2)}) copy-start(bf16[512]{0:T(512)(128)(2,1)} %param.24) | copy-start | bytes 3076
  446.8 12.6 %copy-start.5 = (bf16[512]{0:T(512)(128)(2,1)S(1)}, bf16[512]{0:T(512)(128)(2,1)}, u32[]{:S(2)}) copy-start(bf16[512]{0:T(512)(128)(2,1)} %param.25) | copy-start | bytes 3076
  446.8 12.6 %copy-start.6 = (s32[1,32]{1,0:T(1,128)S(1)}, s32[1,32]{1,0:T(1,128)}, u32[]{:S(2)}) copy-start(s32[1,32]{1,0:T(1,128)} %param.17) | copy-start | bytes 388
  446.8 12.7 %copy-start.3 = (s32[1024]{0:T(1024)S(1)}, s32[1024]{0:T(1024)}, u32[]{:S(2)}) copy-start(s32[1024]{0:T(1024)} %param.16) | copy-start | bytes 12292
  452.9 6.6 %copy-start.1 = (bf16[32,32,512]{2,1,0:T(8,128)(2,1)}, bf16[32,32,512]{2,1,0:T(8,128)(2,1)S(1)}, u32[]{:S(2)}) copy-start(bf16[32,32,512]{2,1,0:T(8,128)(2,1)S(1)} %all-to-all-done.4) | copy-start | bytes 3145732
  452.9 27.9 %all-to-all-start.2 = ((bf16[32,32,512]{2,1,0:T(8,128)(2,1)}), bf16[32,32,512]{2,1,0:T(8,128)(2,1)}, u32[]{:S(2)}, u32[]{:S(2)}) async-start(bf16[32,32,512]{2,1,0:T(8,128)(2,1)} %bitcast.116), calls=%async_computation.2 | async-start | bytes 2097152 | tf_op jit(solution)/shard_map/all_to_all | solution.py:109
Sparse Core Ops, SparseCore 0:
  63.4 36.1 all-gather.17
  127.8 53.6 all-gather.15
  184.1 97.8 all-gather.13
  284.5 71.5 all-gather.11
  358.5 78.3 all-gather.9
